TPU v7x, 32 devices: a whole 2x2x4 slice. The times are simulated.
32 devices in a mesh: node: 16 (over z, y, x), head: 2 (over core).
Axes of the slice: x: 2, y: 2, z: 4, core: 2. Of those that a mesh axis runs over, the one named last changes fastest.
Arguments:
- inputs: bfloat16 [8192, 8192], P('node', 'head'), may hold values from -6 to 6
- b_matrix: bfloat16 [8192, 128], P('node'), may hold values from -0.5390625 to 0.5390625
- c_matrix: bfloat16 [8192, 128], P('node'), may hold values from -0.5390625 to 0.5390625
- step_size: float32 [128, 8192], P('head', 'node'), may hold values from 0 to 4, as said below
- decay_rate: float32 [128], P('head'), may hold values from 0 to 1, as said below
- parents: int32 [16], replicated, may hold values from -1 to 15, as said below
- cotangent: bfloat16 [8192, 8192], P('node', 'head'), may hold values from -0.59765625 to 0.59765625
Outputs:
- outputs: bfloat16 [8192, 8192], P('node', 'head')
- grad_inputs: bfloat16 [8192, 8192], P('node', 'head')
- grad_b: float32 [8192, 128], P(('node', 'head'))
- grad_c: float32 [8192, 128], P(('node', 'head'))
Inputs may be any that keep to these rules, and one draw needn't show every extreme that they name: parents[n] is -1 for a root or the index of another node; following parents from any node reaches a root within 3 steps, and some node is exactly 3 steps from its root. `step_size`: positive. `decay_rate`: positive.
All inputs are finite; a program needn't handle non-finite values.
Results may differ from a plain program's by a relative error of at most 0.019.
Values may be sent and summed in bfloat16 or wider, within the bound.
No kernel may reach another device: no remote copies, remote signals or barrier semaphores. Data moves between devices by JAX's collectives and lax.ppermute only.
A program may use at most 128 MiB of HBM per device.

v0:
```python
import functools
import math

import jax
import jax.numpy as jnp
from jax import lax
from jax.experimental import pallas as pl
from jax.experimental.pallas import tpu as pltpu
from jax.sharding import PartitionSpec as P


LEVELS = 3
VMEM_BYTES = 24 << 20
LANES = 128
SUBLANES = 8
CHUNKS = 2
PARTS = 2

LOG2E = 1.0 / math.log(2.0)

f32 = jnp.float32
bf16 = jnp.bfloat16
NN = (((1,), (0,)), ((), ()))
NT = (((1,), (1,)), ((), ()))


def mm(a, b, dims=NN):
    return lax.dot_general(a, b, dims, preferred_element_type=f32)


def split_two(v):
    high = v.astype(bf16)
    return high, (v - high.astype(f32)).astype(bf16)


def spread_matrix(rows, width, head_width, offset=0):
    row = lax.broadcasted_iota(jnp.int32, (rows, width), 0)
    lane = (lax.broadcasted_iota(jnp.int32, (rows, width), 1) + offset) // head_width
    return (row == lane).astype(bf16)


def head_lanes(columns, first, head_width):
    lane = lax.broadcasted_iota(jnp.int32, columns.shape, 1) // head_width + first
    return jnp.take_along_axis(columns, lane, axis=1)


def pad_lanes(v):
    gap = LANES - v.shape[0]
    if gap:
        v = jnp.concatenate([v, jnp.zeros((gap, v.shape[1]), v.dtype)], axis=0)
    return v.T


def half_steps(step_ref, spread):
    steps = mm(step_ref[...], spread)
    return steps[:1], steps[SUBLANES : SUBLANES + 1]


class Copies:
    def __init__(self, sems):
        self.sems = sems
        self.made = []

    def start(self, source, target):
        copy = pltpu.make_async_copy(source, target, self.sems.at[len(self.made)])
        copy.start()
        self.made.append(copy)
        return copy


def wait_all(copies):
    for copy in copies:
        copy.wait()


def states_kernel(heads, head_width, chunk, block, *refs):
    x_hbm, cot_hbm, b_hbm, c_hbm, step_hbm, rate_hbm = refs[:6]
    outs = refs[6:14]
    x_ref, cot_ref, b_ref, c_ref, step_ref, rate_ref = refs[14:20]
    send_ref, low_ref, src_ref, grow_ref, tail_ref, gram_ref, keep_ref, steps_ref = refs[20:28]
    sems = refs[28]
    length = step_ref.shape[1]
    middle = length // 2
    width = heads * head_width
    count = width // block
    copies = Copies(sems)
    first_in = [
        copies.start(step_hbm.at[pl.ds(chunk * heads, heads)], step_ref),
        copies.start(rate_hbm, rate_ref),
    ]
    later_in = [copies.start(b_hbm, b_ref), copies.start(c_hbm, c_ref)]
    loads = []
    for i in range(count):
        lanes = pl.ds(i * block, block)
        there = pl.ds(chunk * width + i * block, block)
        loads.append(
            [
                copies.start(x_hbm.at[:, there], x_ref.at[:, lanes]),
                copies.start(cot_hbm.at[:, there], cot_ref.at[:, lanes]),
            ]
        )
    wait_all(first_in)
    step = step_ref[...]
    rates = jnp.broadcast_to(rate_ref[...], (LANES, rate_ref.shape[1])).T
    terms = -step * rates[chunk * heads : (chunk + 1) * heads, :1]
    row = lax.broadcasted_iota(jnp.int32, (length, length), 0)
    col = lax.broadcasted_iota(jnp.int32, (length, length), 1)
    upper = (row <= col).astype(bf16)
    first = terms.astype(bf16)
    rest = terms - first.astype(f32)
    second, third = split_two(rest)
    cumulative = mm(third, upper) + mm(second, upper) + mm(first, upper)
    last = cumulative[:, length - 1 :]
    mid = cumulative[:, middle - 1 : middle]
    late = lax.broadcasted_iota(jnp.int32, cumulative.shape, 1) >= middle
    low_ref[...] = pad_lanes(cumulative * LOG2E)
    src_ref[...] = (cumulative - jnp.log(step)) * LOG2E
    grow_ref[...] = pad_lanes(jnp.exp(cumulative - jnp.where(late, mid, 0.0))).astype(bf16)
    tail = jnp.exp(jnp.where(late, last, mid) - cumulative) * step
    tail_ref[...] = pad_lanes(tail).astype(bf16)
    total = jnp.exp(jnp.broadcast_to(last, (heads, send_ref.shape[0])))
    send_ref[:, 2 * width :] = pad_lanes(total).astype(bf16)
    each = (heads, SUBLANES)
    steps = [jnp.broadcast_to(mid, each), jnp.broadcast_to(last - mid, each)]
    steps_ref[...] = pad_lanes(jnp.exp(jnp.concatenate(steps, axis=1))).astype(bf16)
    wait_all(later_in)
    b_turned = b_ref[...].T
    c_turned = c_ref[...].T
    small = (1, 2, 3, 4, 7)
    if chunk == CHUNKS - 1:
        small = (1, 2, 3, 4, 5, 7)
        for rows in (slice(0, middle), slice(middle, length)):
            gram_ref[rows] = mm(c_ref[rows], b_ref[rows], NT).astype(bf16)
    made = (send_ref, low_ref, src_ref, grow_ref, tail_ref, gram_ref, keep_ref, steps_ref)
    stores = []
    ready = [(made[n], outs[n]) for n in small]
    ready.append((send_ref.at[:, pl.ds(2 * width, LANES)], outs[0].at[:, pl.ds(2 * width, LANES)]))
    for i in range(count):
        here = pl.ds(i * block, block)
        there = pl.ds(i * block + width, block)
        wait_all(loads[i])
        spread = spread_matrix(LANES, block, head_width, i * block)
        tailed = mm(tail_ref[...], spread).astype(bf16) * x_ref[:, here]
        emitted = mm(grow_ref[...], spread).astype(bf16) * cot_ref[:, here]
        early_step, late_step = half_steps(steps_ref, spread)
        early_state = mm(b_turned[:, :middle], tailed[:middle])
        late_state = mm(b_turned[:, middle:], tailed[middle:])
        early_seed = mm(c_turned[:, :middle], emitted[:middle])
        late_seed = mm(c_turned[:, middle:], emitted[middle:])
        send_ref[:, here] = (late_step * early_state + late_state).astype(bf16)
        send_ref[:, there] = (early_seed + early_step * late_seed).astype(bf16)
        keep_ref[:, here] = early_state.astype(bf16)
        keep_ref[:, there] = late_seed.astype(bf16)
        stores += [copies.start(*pair) for pair in ready]
        ready = [
            (ref.at[:, lanes], out.at[:, lanes])
            for ref, out in ((send_ref, outs[0]), (keep_ref, outs[6]))
            for lanes in (here, there)
        ]
    stores += [copies.start(*pair) for pair in ready]
    wait_all(stores)


def node_states(x, cot, b, c, step, rate, chunk, heads, head_width):
    length, state = b.shape
    width = heads * head_width
    block = min(width, 4 * LANES)
    count = width // block
    out_shape = [
        jax.ShapeDtypeStruct((state, 2 * width + LANES), bf16),
        jax.ShapeDtypeStruct((length, LANES), f32),
        jax.ShapeDtypeStruct((heads, length), f32),
        jax.ShapeDtypeStruct((length, LANES), bf16),
        jax.ShapeDtypeStruct((length, LANES), bf16),
        jax.ShapeDtypeStruct((length, length // 2), bf16),
        jax.ShapeDtypeStruct((state, 2 * width), bf16),
        jax.ShapeDtypeStruct((2 * SUBLANES, LANES), bf16),
    ]
    held = [(length, width)] * 2 + [b.shape] * 2
    scratch = [pltpu.VMEM(shape, bf16) for shape in held]
    scratch += [pltpu.VMEM((heads, length), f32), pltpu.VMEM(rate.shape, f32)]
    scratch += [pltpu.VMEM(v.shape, v.dtype) for v in out_shape]
    scratch.append(pltpu.SemaphoreType.DMA((11 + 6 * count,)))
    anywhere = pl.BlockSpec(memory_space=pl.ANY)
    return pl.pallas_call(
        functools.partial(states_kernel, heads, head_width, chunk, block),
        in_specs=[anywhere] * 6,
        out_specs=[anywhere] * len(out_shape),
        out_shape=out_shape,
        scratch_shapes=scratch,
        name="node_states",
        cost_estimate=pl.CostEstimate(
            flops=4 * length * state * width,
            bytes_accessed=4 * length * width + 8 * state * width,
            transcendentals=0,
        ),
    )(x, cot, b, c, step, rate)


def inner_kernel(
    head_width,
    first,
    aliased,
    x_ref,
    cot_ref,
    b_ref,
    c_ref,
    given_ref,
    low_ref,
    src_ref,
    *refs,
):
    if aliased:
        refs = refs[2:]
    out_ref, grad_ref, gc_ref, gb_ref, mixed_ref, turned_ref, wa_ref, wb_ref, gram_ref = refs
    length = x_ref.shape[0]
    index = pl.program_id(0)
    pack = LANES // head_width
    pairs = x_ref.shape[1] // LANES
    wide = length // 2
    blocks = wide // LANES
    weights = (wa_ref, wb_ref)

    @pl.when(index == 0)
    def _():
        gram_ref[...] = given_ref[...]
        mixed_ref[...] = jnp.zeros_like(mixed_ref)
        for ref in weights:
            ref[...] = jnp.zeros_like(ref)

    lane = lax.broadcasted_iota(jnp.int32, (1, LANES), 1) // head_width
    causal = lax.broadcasted_iota(jnp.int32, (LANES, LANES), 0) >= lax.broadcasted_iota(
        jnp.int32, (LANES, LANES), 1
    )
    halves = (slice(0, wide), slice(wide, length))
    xs = [x_ref[:, q * LANES : (q + 1) * LANES] for q in range(pairs)]
    turned_cots = [cot_ref[:, q * LANES : (q + 1) * LANES].T for q in range(pairs)]
    low = low_ref[...]

    def decays(h):
        q, a = h // pack, h % pack
        w = weights[h % 2]
        cot = cot_ref[:, q * LANES : (q + 1) * LANES]
        cot = jnp.where(lane == a, cot, jnp.zeros_like(cot))
        place = (first + index * pairs + q) * pack + a
        column = head_lanes(low, place, LANES)
        source = src_ref[pl.ds(place, 1), :]
        for part in halves:
            scores = mm(cot[part], xs[q][part], NT)
            for i in range(blocks):
                here = slice(i * LANES, (i + 1) * LANES)
                rows = slice(part.start + here.start, part.start + here.stop)
                for j in range(i + 1):
                    cols = slice(j * LANES, (j + 1) * LANES)
                    differ = column[rows] - source[:, part.start + cols.start : part.start + cols.stop]
                    if i == j:
                        differ = jnp.where(causal, differ, -jnp.inf)
                    decay = jnp.exp2(differ)
                    w[rows, cols] = decay.astype(bf16) * gram_ref[rows, cols]
                    mixed_ref[rows, cols] += decay * scores[here, cols]
                yield

    def products(h):
        q, a = h // pack, h % pack
        w = weights[h % 2]
        turned = turned_cots[q][a * head_width : (a + 1) * head_width]
        mine = slice(q * LANES + a * head_width, q * LANES + (a + 1) * head_width)
        own = slice(a * head_width, (a + 1) * head_width)
        for part in halves:
            out_ref[part, mine] = mm(w[part], xs[q][part])[:, own].astype(bf16)
            yield
            turned_ref[mine, part] = mm(turned[:, part], w[part]).astype(bf16)
            yield

    def finish(q):
        lanes = slice(q * LANES, (q + 1) * LANES)
        grad_ref[:, lanes] = turned_ref[lanes, :].T

    before = None
    for h in range(pairs * pack):
        for _ in decays(h):
            if before is not None:
                next(before, None)
        if before is not None:
            for _ in before:
                pass
            if h % pack == 0:
                finish(h // pack - 1)
        before = products(h)
    for _ in before:
        pass
    finish(pairs - 1)

    @pl.when(index == pl.num_programs(0) - 1)
    def _():
        for part in halves:
            mixed = mixed_ref[part].astype(bf16)
            gc_ref[part] = mm(mixed, b_ref[part])
            gb_ref[part] = mm(mixed.T, c_ref[part])


def node_inner(x, cot, b, c, gram, low, src, prior, chunk, part, parts, heads, head_width):
    length, state = b.shape
    width = heads * head_width
    block = min(width // parts, 2 * LANES)
    count = width // block // parts
    offset = (chunk * parts + part) * count
    whole = lambda i: (0, 0)
    place = lambda i: (0, offset + i)
    aliased = prior is not None
    operands = [x, cot, b, c, gram, low, src]
    in_specs = [
        pl.BlockSpec((length, block), place),
        pl.BlockSpec((length, block), place),
        pl.BlockSpec((length, state), whole),
        pl.BlockSpec((length, state), whole),
        pl.BlockSpec((length, length // 2), whole),
        pl.BlockSpec((length, LANES), whole),
        pl.BlockSpec((heads, length), whole),
    ]
    aliases = {}
    if aliased:
        aliases = {len(operands): 0, len(operands) + 1: 1}
        operands += list(prior)
        in_specs += [pl.BlockSpec(memory_space=pl.ANY)] * 2
    kernel = functools.partial(inner_kernel, head_width, part * count * block // LANES, aliased)
    return pl.pallas_call(
        kernel,
        grid=(count,),
        in_specs=in_specs,
        out_specs=[
            pl.BlockSpec((length, block), place),
            pl.BlockSpec((length, block), place),
            pl.BlockSpec((length, state), whole),
            pl.BlockSpec((length, state), whole),
        ],
        out_shape=[
            jax.ShapeDtypeStruct(x.shape, bf16),
            jax.ShapeDtypeStruct(x.shape, bf16),
            jax.ShapeDtypeStruct((length, state), f32),
            jax.ShapeDtypeStruct((length, state), f32),
        ],
        scratch_shapes=[
            pltpu.VMEM((length, length // 2), f32),
            pltpu.VMEM((block, length), bf16),
            pltpu.VMEM((length, length // 2), bf16),
            pltpu.VMEM((length, length // 2), bf16),
            pltpu.VMEM((length, length // 2), bf16),
        ],
        input_output_aliases=aliases,
        name="node_inner",
        cost_estimate=pl.CostEstimate(
            flops=24 * length * length * count * block,
            bytes_accessed=12 * length * count * block,
            transcendentals=length * length * heads // parts,
        ),
    )(*operands)


def rank_nodes(parents_ref, rank_ref, half):
    nodes = rank_ref.shape[0]

    def clear(n, carry):
        rank_ref[n] = 0
        return carry

    def mark(n, carry):
        up = parents_ref[n]

        @pl.when(jnp.logical_and(up >= 0, (up >= half) != (n >= half)))
        def _():
            rank_ref[up] = 1

        return carry

    def place(n, count):
        crosses = rank_ref[n]
        rank_ref[n] = jnp.where(crosses > 0, count, -1)
        return count + crosses

    lax.fori_loop(0, nodes, clear, 0)
    lax.fori_loop(0, nodes, mark, 0)
    lax.fori_loop(0, nodes, place, 0)


def widen(narrow, heads, head_width):
    count = narrow.shape[0]
    flat = jnp.concatenate([narrow[n, :1].astype(f32) for n in range(count)], axis=0)
    return mm(flat.astype(bf16), spread_matrix(LANES, heads * head_width, head_width))


def pack_kernel(heads, head_width, parents_ref, recv_ref, *refs):
    tiers, (decay_ref, slot_ref, chain_ref, rank_ref) = refs[:-4], refs[-4:]
    half = recv_ref.shape[0]
    width = heads * head_width
    base = lax.axis_index("node") // half * half
    rank_nodes(parents_ref, rank_ref, half)
    decay_ref[...] = widen(recv_ref[:, :, 2 * width :], heads, head_width)
    slot_ref[...] = jnp.zeros_like(slot_ref)
    chain_ref[...] = jnp.zeros_like(chain_ref)

    def inside(n):
        return jnp.logical_and(n >= base, n < base + half)

    def spot(n):
        return jnp.clip(n - base, 0, half - 1)

    def visit(m, carry):
        node = base + m
        flow = recv_ref[m, :, width : 2 * width].astype(f32)
        at = node
        live = jnp.bool_(True)
        for level in range(LEVELS):
            up = parents_ref[at]
            exists = jnp.logical_and(live, up >= 0)
            live = jnp.logical_and(exists, inside(up))
            away = jnp.logical_and(exists, jnp.logical_not(live))

            @pl.when(away)
            def _(flow=flow, up=up):
                slot = rank_ref[up]
                slot_ref[slot] = slot_ref[slot] + flow

            if level < LEVELS - 1:
                flow = flow * jnp.where(live, decay_ref[pl.ds(spot(up), 1)], 1.0)
            at = jnp.where(live, up, at)

        @pl.when(rank_ref[node] >= 0)
        def _():
            total = recv_ref[m, :, :width].astype(f32)
            factor = decay_ref[pl.ds(m, 1)]
            chain = recv_ref[m, :, 2 * width :].astype(f32)
            at = node
            live = jnp.bool_(True)
            for _ in range(LEVELS - 1):
                up = parents_ref[at]
                live = jnp.logical_and(jnp.logical_and(live, up >= 0), inside(up))
                where = spot(up)
                total = total + jnp.where(live, factor * recv_ref[where, :, :width].astype(f32), 0.0)
                factor = factor * jnp.where(live, decay_ref[pl.ds(where, 1)], 1.0)
                chain = chain * jnp.where(live, recv_ref[where, :, 2 * width :].astype(f32), 1.0)
                at = jnp.where(live, up, at)
            slot_ref[rank_ref[node]] = total
            chain_ref[rank_ref[node]] = chain

        return carry

    lax.fori_loop(0, half, visit, 0)
    at = 0
    for ref in tiers:
        spots = slice(at, at + ref.shape[0])
        ref[:, :, :width] = slot_ref[spots].astype(bf16)
        ref[:, :, width:] = chain_ref[spots].astype(bf16)
        at += ref.shape[0]


def slot_counts(nodes):
    most = nodes * LEVELS // (LEVELS + 1)
    spare = nodes // 8
    return nodes // 2 - spare, spare, most - nodes // 2


def pack_slots(parents, recv, nodes, heads, head_width):
    half, rows, _ = recv.shape
    width = heads * head_width
    counts = slot_counts(nodes)
    in_specs = [pl.BlockSpec(memory_space=pltpu.SMEM), pl.BlockSpec(memory_space=pltpu.VMEM)]
    kernel = functools.partial(pack_kernel, heads, head_width)
    operands = [parents, recv]
    return pl.pallas_call(
        kernel,
        in_specs=in_specs,
        out_specs=[pl.BlockSpec(memory_space=pltpu.VMEM)] * len(counts),
        out_shape=[
            jax.ShapeDtypeStruct((count, rows, width + LANES), bf16) for count in counts
        ],
        scratch_shapes=[
            pltpu.VMEM((half, width), f32),
            pltpu.VMEM((sum(counts), rows, width), f32),
            pltpu.VMEM((sum(counts), rows, LANES), f32),
            pltpu.SMEM((nodes,), jnp.int32),
        ],
        compiler_params=pltpu.CompilerParams(vmem_limit_bytes=VMEM_BYTES),
        name="pack_slots",
        cost_estimate=pl.CostEstimate(
            flops=20 * half * rows * width,
            bytes_accessed=8 * half * rows * width,
            transcendentals=0,
        ),
    )(*operands)


def join_kernel(heads, head_width, parents_ref, recv_ref, *refs):
    tiers = refs[:-6]
    out_ref, decay_ref, slot_ref, chain_ref, back_ref, rank_ref = refs[-6:]
    half = recv_ref.shape[0]
    width = heads * head_width
    base = lax.axis_index("node") // half * half
    rank_nodes(parents_ref, rank_ref, half)
    decay_ref[...] = widen(recv_ref[:, :, 2 * width :], heads, head_width)
    at = 0
    for ref in tiers:
        spots = slice(at, at + ref.shape[0])
        slot_ref[spots] = ref[:, :, :width]
        chain_ref[spots] = widen(ref[:, :, width:], heads, head_width)
        at += ref.shape[0]
    back_ref[...] = jnp.zeros_like(back_ref)

    def inside(n):
        return jnp.logical_and(n >= base, n < base + half)

    def climb(at, flow, start):
        factor = None
        live = jnp.bool_(True)
        for level in range(LEVELS):
            up = parents_ref[at]
            live = jnp.logical_and(live, up >= 0)
            near = jnp.logical_and(live, inside(up))
            far = jnp.logical_and(live, jnp.logical_not(near))
            where = jnp.clip(up - base, 0, half - 1)
            slot = jnp.where(far, rank_ref[jnp.maximum(up, 0)], 0)

            @pl.when(near)
            def _(flow=flow, where=where):
                back_ref[where] = back_ref[where] + flow

            if start is not None:
                value = jnp.where(near, recv_ref[where, :, :width], slot_ref[slot])
                value = jnp.where(live, value.astype(f32), 0.0)
                start = start + (value if factor is None else factor * value)
            if level < LEVELS - 1:
                step = jnp.where(near, decay_ref[pl.ds(where, 1)], chain_ref[pl.ds(slot, 1)])
                flow = flow * step
                factor = step if factor is None else factor * step
                top = jnp.maximum(up, 0)
                for _ in range(LEVELS - 1):
                    above = parents_ref[top]
                    more = jnp.logical_and(far, above >= 0)
                    more = jnp.logical_and(more, jnp.logical_not(inside(above)))
                    top = jnp.where(more, above, top)
                at = top
        return start

    def visit(m, carry):
        node = base + m
        seed = recv_ref[m, :, width : 2 * width].astype(f32)
        start = climb(node, seed, jnp.zeros(seed.shape, f32))
        out_ref[m, :, :width] = start.astype(bf16)

        @pl.when(rank_ref[node] >= 0)
        def _():
            extra = slot_ref[rank_ref[node]].astype(f32)
            back_ref[m] = back_ref[m] + extra
            climb(node, extra * decay_ref[pl.ds(m, 1)], None)

        return carry

    lax.fori_loop(0, half, visit, 0)
    out_ref[:, :, width:] = back_ref[...].astype(bf16)


def join_slots(parents, recv, tiers, nodes, heads, head_width):
    half, rows, _ = recv.shape
    width = heads * head_width
    in_specs = [pl.BlockSpec(memory_space=pltpu.SMEM)] + [
        pl.BlockSpec(memory_space=pltpu.VMEM)
    ] * (1 + len(tiers))
    kernel = functools.partial(join_kernel, heads, head_width)
    operands = [parents, recv, *tiers]
    slots = sum(v.shape[0] for v in tiers)
    return pl.pallas_call(
        kernel,
        in_specs=in_specs,
        out_specs=pl.BlockSpec(memory_space=pltpu.VMEM),
        out_shape=jax.ShapeDtypeStruct((half, rows, 2 * width), bf16),
        scratch_shapes=[
            pltpu.VMEM((half, width), f32),
            pltpu.VMEM((slots, rows, width), bf16),
            pltpu.VMEM((slots, width), f32),
            pltpu.VMEM((half, rows, width), f32),
            pltpu.SMEM((nodes,), jnp.int32),
        ],
        compiler_params=pltpu.CompilerParams(vmem_limit_bytes=VMEM_BYTES),
        name="join_slots",
        cost_estimate=pl.CostEstimate(
            flops=20 * half * rows * width,
            bytes_accessed=8 * half * rows * width,
            transcendentals=0,
        ),
    )(*operands)


def outer_kernel(heads, head_width, chunk, block, extras, final, *refs):
    given = 13 + 2 * extras
    sources = refs[:given]
    refs = refs[given:]
    if final:
        outs, owns, pieces = refs[2:4], refs[4:6], refs[6 : -(given + 5)]
        gc_ref, gb_ref = refs[-2:]
        refs = refs[-(given + 5) : -2]
    else:
        outs, (gc_ref, gb_ref) = refs[:2], refs[2:4]
        refs = refs[4:]
    held, results, sems = refs[:given], refs[given : given + 2], refs[-1]
    b_ref, c_ref, grow_ref, tail_ref, step_ref = held[:5]
    added = held[5 : 5 + 2 * extras]
    x_ref, cot_ref, inner_ref, grad_ref, start_ref, back_ref, early_ref, late_ref = held[-8:]
    width = heads * head_width
    count = width // block
    middle = x_ref.shape[0] // 2
    copies = Copies(sems)
    small = [copies.start(sources[n], held[n]) for n in range(5)]
    loads = []
    for i in range(count):
        lanes = pl.ds(i * block, block)
        over = pl.ds(width + i * block, block)
        column = pl.ds(chunk * width + i * block, block)
        spots = (column,) * 4 + (lanes, over) * 2
        loads.append(
            [
                copies.start(source.at[:, spot], ref.at[:, lanes])
                for source, spot, ref in zip(sources[-8:], spots, held[-8:])
            ]
        )
    sums = [copies.start(sources[5 + n], ref) for n, ref in enumerate(added)]
    wait_all(small)
    stores = []
    ready = []
    for i in range(count):
        here = pl.ds(i * block, block)
        column = pl.ds(chunk * width + i * block, block)
        wait_all(loads[i])
        spread = spread_matrix(LANES, block, head_width, i * block)
        grow_wide = mm(grow_ref[...], spread)
        tail_wide = mm(tail_ref[...], spread)
        early_step, late_step = half_steps(step_ref, spread)
        start = start_ref[:, here]
        back = back_ref[:, here]
        after = (early_step * start.astype(f32) + early_ref[:, here].astype(f32)).astype(bf16)
        before = (late_step * back.astype(f32) + late_ref[:, here].astype(f32)).astype(bf16)
        for n, part in enumerate((slice(0, middle), slice(middle, 2 * middle))):
            grow = grow_wide[part]
            tail = tail_wide[part]
            begin = (start, after)[n]
            end = (before, back)[n]
            carried = grow * mm(c_ref[part], begin)
            results[0][part, here] = (inner_ref[part, here].astype(f32) + carried).astype(bf16)
            carried = tail * mm(b_ref[part], end)
            results[1][part, here] = (grad_ref[part, here].astype(f32) + carried).astype(bf16)
            gc = mm(grow.astype(bf16) * cot_ref[part, here], begin, NT)
            gb = mm(tail.astype(bf16) * x_ref[part, here], end, NT)
            if i == 0:
                gc_ref[part] = gc
                gb_ref[part] = gb
            else:
                gc_ref[part] += gc
                gb_ref[part] += gb
        stores += [copies.start(*pair) for pair in ready]
        ready = [
            (result.at[:, here], out.at[:, column]) for result, out in zip(results, outs)
        ]
    wait_all(sums)
    gc_ref[...] += sum(ref[...] for ref in added[:extras])
    gb_ref[...] += sum(ref[...] for ref in added[extras:])
    stores += [copies.start(*pair) for pair in ready]
    if final:
        size = len(pieces) + 1
        me = lax.axis_index("head")
        rows = owns[0].shape[0]
        for shift in range(size):
            at = pl.multiple_of(lax.rem(me + shift, size) * rows, rows)
            for n, ref in enumerate((gb_ref, gc_ref)):
                if shift == 0:
                    owns[n][...] = ref[pl.ds(at, rows)]
                else:
                    pieces[shift - 1][n] = ref[pl.ds(at, rows)].astype(bf16)
    wait_all(stores)


def node_outer(
    x, cot, b, c, grow, tail, states, keep, steps, inner, grad, found, prior, chunk, heads, head_width
):
    length, state = b.shape
    width = heads * head_width
    block = min(width, 4 * LANES)
    count = width // block
    final = prior is not None
    small = [b, c, grow, tail, steps] + [v[1] for v in found] + [v[0] for v in found]
    operands = small + [x, cot, inner, grad, states, states, keep, keep]
    given = len(operands)
    anywhere = pl.BlockSpec(memory_space=pl.ANY)
    local = pl.BlockSpec(memory_space=pltpu.VMEM)
    out_specs = [anywhere] * 2
    out_shape = [jax.ShapeDtypeStruct(x.shape, bf16)] * 2
    scratch = [pltpu.VMEM(v.shape, v.dtype) for v in small]
    scratch += [pltpu.VMEM((length, width), bf16)] * 4 + [pltpu.VMEM((state, width), bf16)] * 4
    scratch += [pltpu.VMEM((length, width), bf16)] * 2
    scratch.append(pltpu.SemaphoreType.DMA((len(small) + 10 * count,)))
    aliases = {}
    if final:
        aliases = {given: 0, given + 1: 1}
        operands += list(prior)
        size = lax.axis_size("head")
        kept = (2, length // size, state)
        out_specs += [local] * (size + 1)
        out_shape += [jax.ShapeDtypeStruct(kept[1:], f32)] * 2
        out_shape += [jax.ShapeDtypeStruct(kept, bf16)] * (size - 1)
        scratch += [pltpu.VMEM((length, state), f32)] * 2
    else:
        out_specs += [local] * 2
        out_shape += [jax.ShapeDtypeStruct((length, state), f32)] * 2
    return pl.pallas_call(
        functools.partial(outer_kernel, heads, head_width, chunk, block, len(found), final),
        in_specs=[anywhere] * len(operands),
        out_specs=out_specs,
        out_shape=out_shape,
        scratch_shapes=scratch,
        input_output_aliases=aliases,
        name="node_outer",
        cost_estimate=pl.CostEstimate(
            flops=8 * length * state * width,
            bytes_accessed=14 * length * width,
            transcendentals=0,
        ),
    )(*operands)


def scatter_sum(owns, pieces):
    size = lax.axis_size("head")
    for shift, piece in enumerate(pieces, 1):
        pairs = [(i, (i + shift) % size) for i in range(size)]
        moved = lax.ppermute(piece, "head", pairs).astype(f32)
        owns = [own + moved[n] for n, own in enumerate(owns)]
    return owns


def one_device(inputs, b_matrix, c_matrix, step_size, decay_rate, parents, cotangent):
    state = b_matrix.shape[1]
    head_count = step_size.shape[0]
    head_width = inputs.shape[1] // head_count
    nodes = lax.axis_size("node")
    heads = head_count // CHUNKS
    half = nodes // 2
    rate = decay_rate[None, :]
    groups = [list(range(half)), list(range(half, nodes))]
    across = [(n, (n + half) % nodes) for n in range(nodes)]

    def swap(v):
        return lax.all_to_all(
            v.reshape(half, state // half, v.shape[-1]),
            "node",
            split_axis=0,
            concat_axis=0,
            tiled=True,
            axis_index_groups=groups,
        )

    def cross(v):
        return lax.ppermute(v, "node", across)

    places = jnp.arange(nodes)
    child = jnp.logical_and(
        parents[:, None] == places[None, :],
        (places[:, None] < half) != (places[None, :] < half),
    )
    crossing = jnp.sum(jnp.any(child, axis=0).astype(jnp.int32))
    always, spare, _ = slot_counts(nodes)
    crowded = (crossing > always).astype(jnp.int32) + (crossing > always + spare)

    shared = (inputs, cotangent, b_matrix, c_matrix)
    sizes = (heads, head_width)
    made = []
    for k in range(CHUNKS):
        made.append(node_states(*shared, step_size, rate, k, *sizes))
    received = [swap(made[k][0]) for k in range(CHUNKS)]
    found = []
    prior = None
    for k in range(CHUNKS):
        for part in range(PARTS):
            *prior, gc, gb = node_inner(
                *shared, made[-1][5], made[k][1], made[k][2], prior, k, part, PARTS, *sizes
            )
            found.append((gb, gc))
    inner = prior
    packed = []
    for k in range(CHUNKS):
        main, *more = pack_slots(parents, received[k], nodes, *sizes)
        held = pltpu.with_memory_space_constraint(main, pltpu.HBM)
        packed.append((cross(held), more))
    others = lax.switch(
        crowded,
        (
            lambda vs: vs,
            lambda vs: [(cross(v[0]), v[1]) for v in vs],
            lambda vs: [(cross(v[0]), cross(v[1])) for v in vs],
        ),
        [tuple(p[1]) for p in packed],
    )
    states = []
    for k in range(CHUNKS):
        tiers = (packed[k][0], *others[k])
        joined = join_slots(parents, received[k], tiers, nodes, *sizes)
        states.append(swap(joined).reshape(state, -1))
    prior = None
    for k in range(CHUNKS):
        result = node_outer(
            *shared, *made[k][3:5], states[k], *made[k][6:8], *inner, found, prior, k, *sizes
        )
        prior = result[:2]
        if k == 0:
            found = [(result[3], result[2])]
    grads = scatter_sum(result[2:4], result[4:])
    return prior[0], prior[1], grads[0], grads[1]


def solution(mesh):
    return jax.shard_map(
        one_device,
        mesh=mesh,
        in_specs=(
            P("node", "head"),
            P("node", None),
            P("node", None),
            P("head", "node"),
            P("head"),
            P(),
            P("node", "head"),
        ),
        out_specs=(
            P("node", "head"),
            P("node", "head"),
            P(("node", "head"), None),
            P(("node", "head"), None),
        ),
        check_vma=False,
    )
```

profile of v0, /device:TPU:0, one launch (start us, length us, event | category | flops | bytes accessed | tf_op | source)
XLA Modules:
  0.0 153.2 jit_solution(6894237106663756068)
XLA Ops:
  0.6 5.5 %node_states.3 = (bf16[128,4224]{1,0:T(8,128)(2,1)}, f32[512,128]{1,0:T(8,128)}, f32[32,512]{1,0:T(8,128)}, bf16[512,128]{1,0:T(8,128)(2,1)}, bf16[512,128]{1,0:...) custom-call(bf16[512,4096]{1,0:T(8,128)(2,1)} %refs_7_.1, ...), custom_call_target="tpu_custom_call" | custom-call | flops 536870912 | bytes 6291456 | tf_op jit(solution)/shard_map/node_states/pallas_call | solution.py:185
  6.1 6.2 %all-to-all-start = ((bf16[8,16,4224]{2,1,0:T(8,128)(2,1)}), bf16[8,16,4224]{2,1,0:T(8,128)(2,1)S(1)}, u32[]{:S(2)}, u32[]{:S(2)}) async-start(bf16[8,16,4224]{2,1,0:T(8,128)(2,1)} %bitcast.18), calls=%async_computation | async-start | bytes 2162688 | tf_op jit(solution)/shard_map/all_to_all | solution.py:749
  12.3 5.7 %node_states.2 = (bf16[128,4224]{1,0:T(8,128)(2,1)}, f32[512,128]{1,0:T(8,128)}, f32[32,512]{1,0:T(8,128)}, bf16[512,128]{1,0:T(8,128)(2,1)}, bf16[512,128]{1,0:...) custom-call(bf16[512,4096]{1,0:T(8,128)(2,1)} %refs_7_.1, ...), custom_call_target="tpu_custom_call" | custom-call | flops 536870912 | bytes 6291456 | tf_op jit(solution)/shard_map/node_states/pallas_call | solution.py:185
  18.0 9.4 %all-to-all-done.recv_ref = bf16[8,16,4224]{2,1,0:T(8,128)(2,1)S(1)} async-done(((bf16[8,16,4224]{2,1,0:T(8,128)(2,1)}), bf16[8,16,4224]{2,1,0:T(8,128)(2,1)S(1)}, u32[]{:S(2)}, u32[]{:S(2)}) %all-to-all-start) | async-done | bytes 1081376 | tf_op jit(solution)/shard_map/all_to_all | solution.py:749
  27.4 3.6 %all-to-all-start.1 = ((bf16[8,16,4224]{2,1,0:T(8,128)(2,1)}), bf16[8,16,4224]{2,1,0:T(8,128)(2,1)S(1)}, u32[]{:S(2)}, u32[]{:S(2)}) async-start(bf16[8,16,4224]{2,1,0:T(8,128)(2,1)} %bitcast.17), calls=%async_computation.1 | async-start | bytes 2162688 | tf_op jit(solution)/shard_map/all_to_all | solution.py:749
  31.0 2.5 %pack_slots.2 = (bf16[6,16,2176]{2,1,0:T(8,128)(2,1)S(1)}, bf16[2,16,2176]{2,1,0:T(8,128)(2,1)}, bf16[4,16,2176]{2,1,0:T(8,128)(2,1)}) custom-call(s32[16]{0:T(128)S(1)} %copy-done, bf16[8,16,4224]{2,1,0:T(8,128)(2,1)S(1)} %all-to-all-done.recv_ref), custom_call_target="tpu_custom_call" | custom-call | flops 5242880 | bytes 2097152 | tf_op jit(solution)/shard_map/pack_slots/pallas_call | solution.py:470
  33.5 2.7 %collective-permute-start.6 = (bf16[6,16,2176]{2,1,0:T(8,128)(2,1)S(1)}, bf16[6,16,2176]{2,1,0:T(8,128)(2,1)S(1)}, u32[]{:S(2)}, u32[]{:S(2)}) collective-permute-start(bf16[6,16,2176]{2,1,0:T(8,128)(2,1)S(1)} %get-tuple-element.114), channel_id=1, source_target_pairs={{0,16},{2,18},{4,20},{6,22},{8,24},{10,26},{12,28},{14,30},{16,0},... | collective-permute-start | bytes 1253384 | tf_op jit(solution)/shard_map/ppermute | solution.py:759
  38.2 15.9 %all-to-all-done.1.recv_ref = bf16[8,16,4224]{2,1,0:T(8,128)(2,1)S(1)} async-done(((bf16[8,16,4224]{2,1,0:T(8,128)(2,1)}), bf16[8,16,4224]{2,1,0:T(8,128)(2,1)S(1)}, u32[]{:S(2)}, u32[]{:S(2)}) %all-to-all-start.1) | async-done | bytes 1081376 | tf_op jit(solution)/shard_map/all_to_all | solution.py:749
  54.1 2.6 %pack_slots.3 = (bf16[6,16,2176]{2,1,0:T(8,128)(2,1)S(1)}, bf16[2,16,2176]{2,1,0:T(8,128)(2,1)}, bf16[4,16,2176]{2,1,0:T(8,128)(2,1)}) custom-call(s32[16]{0:T(128)S(1)} %copy-done, bf16[8,16,4224]{2,1,0:T(8,128)(2,1)S(1)} %all-to-all-done.1.recv_ref), custom_call_target="tpu_custom_call" | custom-call | flops 5242880 | bytes 2097152 | tf_op jit(solution)/shard_map/pack_slots/pallas_call | solution.py:470
  56.6 13.7 %conditional.1 = ((bf16[2,16,2176]{2,1,0:T(8,128)(2,1)}, bf16[4,16,2176]{2,1,0:T(8,128)(2,1)}, bf16[2,16,2176]{2,1,0:T(8,128)(2,1)}, bf16[4,16,2176]{2,1,0:T(8,128)(2,1)})) conditional(s32[]{:T(128)} %clamp.3, (bf16[2,16,2176]{2,1,0:T(8,128)(2,1)}, bf16[4,16,2176]{2,1,0:T(8,128)(2,1)}, bf16[2,16,2176]{2,1,0:T(8,128)(2,1)}, ...), branch_computations={%region_2.0_spmd, %region_3.0_spmd, %region_4.0_spmd} | conditional | bytes 5013704 | solution.py:790
  56.7 2.9 %collective-permute-start.1 = (bf16[2,16,2176]{2,1,0:T(8,128)(2,1)}, bf16[2,16,2176]{2,1,0:T(8,128)(2,1)S(1)}, u32[]{:S(2)}, u32[]{:S(2)}) collective-permute-start(bf16[2,16,2176]{2,1,0:T(8,128)(2,1)} %get-tuple-element.26), channel_id=1, source_target_pairs={{0,16},{2,18},{4,20},{6,22},{8,24},{10,26},{12,28},{14,30},{16,0},... | collective-permute-start | bytes 417800 | tf_op jit(solution)/shard_map/cond/branch_1_fun/ppermute | solution.py:759
  59.6 7.3 %collective-permute-done = bf16[2,16,2176]{2,1,0:T(8,128)(2,1)S(1)} collective-permute-done((bf16[2,16,2176]{2,1,0:T(8,128)(2,1)}, bf16[2,16,2176]{2,1,0:T(8,128)(2,1)S(1)}, u32[]{:S(2)}, u32[]{:S(2)}) %collective-permute-start) | collective-permute-done | bytes 139296 | tf_op jit(solution)/shard_map/cond/branch_1_fun/ppermute | solution.py:759
  66.8 0.7 copy.29
  67.5 2.2 %collective-permute-done.1 = bf16[2,16,2176]{2,1,0:T(8,128)(2,1)S(1)} collective-permute-done((bf16[2,16,2176]{2,1,0:T(8,128)(2,1)}, bf16[2,16,2176]{2,1,0:T(8,128)(2,1)S(1)}, u32[]{:S(2)}, u32[]{:S(2)}) %collective-permute-start.1) | collective-permute-done | bytes 139296 | tf_op jit(solution)/shard_map/cond/branch_1_fun/ppermute | solution.py:759
  69.7 0.6 copy.31
  70.4 0.8 copy-done.3
  71.1 3.9 %join_slots.2 = bf16[8,16,4096]{2,1,0:T(8,128)(2,1)} custom-call(s32[16]{0:T(128)S(1)} %copy-done, bf16[8,16,4224]{2,1,0:T(8,128)(2,1)S(1)} %all-to-all-done.recv_ref, bf16[6,16,2176]{2,1,0:T(8,128)(2,1)} %copy-done.3, bf16[2,16,2176]{2,1,0:T(8,128)(2,1)} %get-tuple-element.120.refs_1_, bf16[4,16,2176]{2,1,0:T(8,128)(2,1)} %get-tuple-element.121.refs_2_), custom_call_target="tpu_custom_call" | custom-call | flops 5242880 | bytes 2097152 | tf_op jit(solution)/shard_map/join_slots/pallas_call | solution.py:571
  75.1 3.6 %all-to-all-start.2 = ((bf16[8,16,4096]{2,1,0:T(8,128)(2,1)}), bf16[8,16,4096]{2,1,0:T(8,128)(2,1)S(1)}, u32[]{:S(2)}, u32[]{:S(2)}) async-start(bf16[8,16,4096]{2,1,0:T(8,128)(2,1)} %join_slots.2), calls=%async_computation.2 | async-start | bytes 2097152 | tf_op jit(solution)/shard_map/all_to_all | solution.py:749
  78.7 1.8 %collective-permute-start.7 = (bf16[6,16,2176]{2,1,0:T(8,128)(2,1)S(1)}, bf16[6,16,2176]{2,1,0:T(8,128)(2,1)S(1)}, u32[]{:S(2)}, u32[]{:S(2)}) collective-permute-start(bf16[6,16,2176]{2,1,0:T(8,128)(2,1)S(1)} %get-tuple-element.125), channel_id=1, source_target_pairs={{0,16},{2,18},{4,20},{6,22},{8,24},{10,26},{12,28},{14,30},{16,0},... | collective-permute-start | bytes 1253384 | tf_op jit(solution)/shard_map/ppermute | solution.py:759
  80.5 6.9 %node_inner.4 = (bf16[512,4096]{1,0:T(8,128)(2,1)}, bf16[512,4096]{1,0:T(8,128)(2,1)}, f32[512,128]{1,0:T(8,128)}, f32[512,128]{1,0:T(8,128)}) custom-call(bf16[512,4096]{1,0:T(8,128)(2,1)} %refs_7_.1, bf16[512,4096]{1,0:T(8,128)(2,1)} %refs_8_.1, bf16[512,128]{1,0:T(8,128)(2,1)} %refs_0_.7, bf16[512,128]{1,0:T(8,128)(2,1)} %refs_1_.7, ...), custom_call_target="tpu_custom_call" | custom-call | flops 6442450944 | bytes 6291456 | tf_op jit(solution)/shard_map/node_inner/pallas_call | solution.py:327
  87.4 12.1 %collective-permute-done.7.refs_0_ = bf16[6,16,2176]{2,1,0:T(8,128)(2,1)S(1)} collective-permute-done((bf16[6,16,2176]{2,1,0:T(8,128)(2,1)S(1)}, bf16[6,16,2176]{2,1,0:T(8,128)(2,1)S(1)}, u32[]{:S(2)}, u32[]{:S(2)}) %collective-permute-start.7) | collective-permute-done | bytes 417824 | tf_op jit(solution)/shard_map/ppermute | solution.py:759
  99.5 0.8 copy-done.4
  100.2 3.8 %join_slots.3 = bf16[8,16,4096]{2,1,0:T(8,128)(2,1)} custom-call(s32[16]{0:T(128)S(1)} %copy-done, bf16[8,16,4224]{2,1,0:T(8,128)(2,1)S(1)} %all-to-all-done.1.recv_ref, bf16[6,16,2176]{2,1,0:T(8,128)(2,1)} %copy-done.4, bf16[2,16,2176]{2,1,0:T(8,128)(2,1)S(1)} %copy-done.6, bf16[4,16,2176]{2,1,0:T(8,128)(2,1)S(1)} %copy-done.5), custom_call_target="tpu_custom_call" | custom-call | flops 5242880 | bytes 2097152 | tf_op jit(solution)/shard_map/join_slots/pallas_call | solution.py:571
  104.0 6.1 %all-to-all-start.3 = ((bf16[8,16,4096]{2,1,0:T(8,128)(2,1)}), bf16[8,16,4096]{2,1,0:T(8,128)(2,1)S(1)}, u32[]{:S(2)}, u32[]{:S(2)}) async-start(bf16[8,16,4096]{2,1,0:T(8,128)(2,1)} %join_slots.3), calls=%async_computation.3 | async-start | bytes 2097152 | tf_op jit(solution)/shard_map/all_to_all | solution.py:749
  110.2 6.8 %node_inner.5 = (bf16[512,4096]{1,0:T(8,128)(2,1)}, bf16[512,4096]{1,0:T(8,128)(2,1)}, f32[512,128]{1,0:T(8,128)}, f32[512,128]{1,0:T(8,128)}) custom-call(bf16[512,4096]{1,0:T(8,128)(2,1)} %refs_7_.1, bf16[512,4096]{1,0:T(8,128)(2,1)} %refs_8_.1, bf16[512,128]{1,0:T(8,128)(2,1)} %refs_0_.7, ...), custom_call_target="tpu_custom_call", output_to_operand_aliasing={{0}: (7, {}), {1}: (8, {})} | custom-call | flops 6442450944 | bytes 6291456 | tf_op jit(solution)/shard_map/node_inner/pallas_call | solution.py:327
  117.0 6.9 %node_inner.6 = (bf16[512,4096]{1,0:T(8,128)(2,1)}, bf16[512,4096]{1,0:T(8,128)(2,1)}, f32[512,128]{1,0:T(8,128)}, f32[512,128]{1,0:T(8,128)}) custom-call(bf16[512,4096]{1,0:T(8,128)(2,1)} %refs_7_.1, bf16[512,4096]{1,0:T(8,128)(2,1)} %refs_8_.1, bf16[512,128]{1,0:T(8,128)(2,1)} %refs_0_.7, ...), custom_call_target="tpu_custom_call", output_to_operand_aliasing={{0}: (7, {}), {1}: (8, {})} | custom-call | flops 6442450944 | bytes 6291456 | tf_op jit(solution)/shard_map/node_inner/pallas_call | solution.py:327
  123.9 6.9 %node_inner.7 = (bf16[512,4096]{1,0:T(8,128)(2,1)}, bf16[512,4096]{1,0:T(8,128)(2,1)}, f32[512,128]{1,0:T(8,128)}, f32[512,128]{1,0:T(8,128)}) custom-call(bf16[512,4096]{1,0:T(8,128)(2,1)} %refs_7_.1, bf16[512,4096]{1,0:T(8,128)(2,1)} %refs_8_.1, bf16[512,128]{1,0:T(8,128)(2,1)} %refs_0_.7, ...), custom_call_target="tpu_custom_call", output_to_operand_aliasing={{0}: (7, {}), {1}: (8, {})} | custom-call | flops 6442450944 | bytes 6291456 | tf_op jit(solution)/shard_map/node_inner/pallas_call | solution.py:327
  130.9 9.0 %node_outer.2 = (bf16[512,4096]{1,0:T(8,128)(2,1)}, bf16[512,4096]{1,0:T(8,128)(2,1)}, f32[512,128]{1,0:T(8,128)}, f32[512,128]{1,0:T(8,128)}) custom-call(bf16[512,128]{1,0:T(8,128)(2,1)} %refs_0_.7, bf16[512,128]{1,0:T(8,128)(2,1)} %refs_1_.7, bf16[512,128]{1,0:T(8,128)(2,1)} %get-tuple-element.89.refs_2_, bf16[512,128]{1,0:T(8,128)(2,1)} %get-tuple-element.90.refs_3_, ...), custom_call_target="tpu_custom_call" | custom-call | flops 1073741824 | bytes 14680064 | tf_op jit(solution)/shard_map/node_outer/pallas_call | solution.py:712
  139.9 1.0 copy-done.2
  140.9 8.9 %node_outer.3 = (bf16[512,4096]{1,0:T(8,128)(2,1)}, bf16[512,4096]{1,0:T(8,128)(2,1)}, f32[256,128]{1,0:T(8,128)}, f32[256,128]{1,0:T(8,128)}, bf16[2,256,128]{2,1,0:T(8,128)(2,1)}) custom-call(bf16[512,128]{1,0:T(8,128)(2,1)} %refs_0_.7, bf16[512,128]{1,0:T(8,128)(2,1)} %refs_1_.7, ...), custom_call_target="tpu_custom_call", output_to_operand_aliasing={{0}: (15, {}), {1}: (16, {})} | custom-call | flops 1073741824 | bytes 14680064 | tf_op jit(solution)/shard_map/node_outer/pallas_call | solution.py:712
  149.9 1.5 %collective-permute-done.8 = bf16[2,256,128]{2,1,0:T(8,128)(2,1)S(1)} collective-permute-done((bf16[2,256,128]{2,1,0:T(8,128)(2,1)}, bf16[2,256,128]{2,1,0:T(8,128)(2,1)S(1)}, u32[]{:S(2)}, u32[]{:S(2)}) %collective-permute-start.8) | collective-permute-done | bytes 131104 | tf_op jit(solution)/shard_map/ppermute | solution.py:732
  151.5 1.7 %fusion = (f32[256,128]{1,0:T(8,128)}, f32[256,128]{1,0:T(8,128)}) fusion(f32[256,128]{1,0:T(8,128)} %get-tuple-element.135, f32[2,256,128]{2,1,0:T(8,128)S(1)} %convert_element_type.15, f32[256,128]{1,0:T(8,128)} %get-tuple-element.133), kind=kLoop, calls=%fused_computation.1 | loop fusion | flops 65536 | bytes 786432 | tf_op jit(solution)/shard_map/add | solution.py:733
  (20 shorter events, 0.9 us)
Async XLA Ops:
  6.1 21.3 %all-to-all-start = ((bf16[8,16,4224]{2,1,0:T(8,128)(2,1)}), bf16[8,16,4224]{2,1,0:T(8,128)(2,1)S(1)}, u32[]{:S(2)}, u32[]{:S(2)}) async-start(bf16[8,16,4224]{2,1,0:T(8,128)(2,1)} %bitcast.18), calls=%async_computation | async-start | bytes 2162688 | tf_op jit(solution)/shard_map/all_to_all | solution.py:749
  12.3 18.6 %copy-start = (s32[16]{0:T(128)S(1)}, s32[16]{0:T(128)}, u32[]{:S(2)}) copy-start(s32[16]{0:T(128)} %parents_ref.7) | copy-start | bytes 196
  27.4 26.7 %all-to-all-start.1 = ((bf16[8,16,4224]{2,1,0:T(8,128)(2,1)}), bf16[8,16,4224]{2,1,0:T(8,128)(2,1)S(1)}, u32[]{:S(2)}, u32[]{:S(2)}) async-start(bf16[8,16,4224]{2,1,0:T(8,128)(2,1)} %bitcast.17), calls=%async_computation.1 | async-start | bytes 2162688 | tf_op jit(solution)/shard_map/all_to_all | solution.py:749
  33.5 36.9 %collective-permute-start.6 = (bf16[6,16,2176]{2,1,0:T(8,128)(2,1)S(1)}, bf16[6,16,2176]{2,1,0:T(8,128)(2,1)S(1)}, u32[]{:S(2)}, u32[]{:S(2)}) collective-permute-start(bf16[6,16,2176]{2,1,0:T(8,128)(2,1)S(1)} %get-tuple-element.114), channel_id=1, source_target_pairs={{0,16},{2,18},{4,20},{6,22},{8,24},{10,26},{12,28},{14,30},{16,0},... | collective-permute-start | bytes 1253384 | tf_op jit(solution)/shard_map/ppermute | solution.py:759
  56.6 10.2 %collective-permute-start = (bf16[2,16,2176]{2,1,0:T(8,128)(2,1)}, bf16[2,16,2176]{2,1,0:T(8,128)(2,1)S(1)}, u32[]{:S(2)}, u32[]{:S(2)}) collective-permute-start(bf16[2,16,2176]{2,1,0:T(8,128)(2,1)} %get-tuple-element.24), channel_id=1, source_target_pairs={{0,16},{2,18},{4,20},{6,22},{8,24},{10,26},{12,28},{14,30},{16,0},... | collective-permute-start | bytes 417800 | tf_op jit(solution)/shard_map/cond/branch_1_fun/ppermute | solution.py:759
  56.7 13.1 %collective-permute-start.1 = (bf16[2,16,2176]{2,1,0:T(8,128)(2,1)}, bf16[2,16,2176]{2,1,0:T(8,128)(2,1)S(1)}, u32[]{:S(2)}, u32[]{:S(2)}) collective-permute-start(bf16[2,16,2176]{2,1,0:T(8,128)(2,1)} %get-tuple-element.26), channel_id=1, source_target_pairs={{0,16},{2,18},{4,20},{6,22},{8,24},{10,26},{12,28},{14,30},{16,0},... | collective-permute-start | bytes 417800 | tf_op jit(solution)/shard_map/cond/branch_1_fun/ppermute | solution.py:759
  70.4 0.8 copy-start.3
  75.1 29.0 %all-to-all-start.2 = ((bf16[8,16,4096]{2,1,0:T(8,128)(2,1)}), bf16[8,16,4096]{2,1,0:T(8,128)(2,1)S(1)}, u32[]{:S(2)}, u32[]{:S(2)}) async-start(bf16[8,16,4096]{2,1,0:T(8,128)(2,1)} %join_slots.2), calls=%async_computation.2 | async-start | bytes 2097152 | tf_op jit(solution)/shard_map/all_to_all | solution.py:749
  78.7 20.8 %collective-permute-start.7 = (bf16[6,16,2176]{2,1,0:T(8,128)(2,1)S(1)}, bf16[6,16,2176]{2,1,0:T(8,128)(2,1)S(1)}, u32[]{:S(2)}, u32[]{:S(2)}) collective-permute-start(bf16[6,16,2176]{2,1,0:T(8,128)(2,1)S(1)} %get-tuple-element.125), channel_id=1, source_target_pairs={{0,16},{2,18},{4,20},{6,22},{8,24},{10,26},{12,28},{14,30},{16,0},... | collective-permute-start | bytes 1253384 | tf_op jit(solution)/shard_map/ppermute | solution.py:759
  80.5 19.7 %copy-start.5 = (bf16[4,16,2176]{2,1,0:T(8,128)(2,1)S(1)}, bf16[4,16,2176]{2,1,0:T(8,128)(2,1)}, u32[]{:S(2)}) copy-start(bf16[4,16,2176]{2,1,0:T(8,128)(2,1)} %get-tuple-element.127.refs_2_) | copy-start | bytes 835588
  80.5 19.8 %copy-start.6 = (bf16[2,16,2176]{2,1,0:T(8,128)(2,1)S(1)}, bf16[2,16,2176]{2,1,0:T(8,128)(2,1)}, u32[]{:S(2)}) copy-start(bf16[2,16,2176]{2,1,0:T(8,128)(2,1)} %get-tuple-element.126.refs_1_) | copy-start | bytes 417796
  99.5 0.8 copy-start.4
  104.0 13.0 %copy-start.1 = (bf16[8,16,4096]{2,1,0:T(8,128)(2,1)}, bf16[8,16,4096]{2,1,0:T(8,128)(2,1)S(1)}, u32[]{:S(2)}) copy-start(bf16[8,16,4096]{2,1,0:T(8,128)(2,1)S(1)} %all-to-all-done.2) | copy-start | bytes 3145732
  104.0 35.9 %all-to-all-start.3 = ((bf16[8,16,4096]{2,1,0:T(8,128)(2,1)}), bf16[8,16,4096]{2,1,0:T(8,128)(2,1)S(1)}, u32[]{:S(2)}, u32[]{:S(2)}) async-start(bf16[8,16,4096]{2,1,0:T(8,128)(2,1)} %join_slots.3), calls=%async_computation.3 | async-start | bytes 2097152 | tf_op jit(solution)/shard_map/all_to_all | solution.py:749
  139.9 1.0 copy-start.2
  149.8 1.6 %collective-permute-start.8 = (bf16[2,256,128]{2,1,0:T(8,128)(2,1)}, bf16[2,256,128]{2,1,0:T(8,128)(2,1)S(1)}, u32[]{:S(2)}, u32[]{:S(2)}) collective-permute-start(bf16[2,256,128]{2,1,0:T(8,128)(2,1)} %get-tuple-element.134), channel_id=1, source_target_pairs={{0,1},{1,0},{2,3},{3,2},{4,5},{5,4},{6,7},{7,6},{8,9},{9,8},{10,11... | collective-permute-start | bytes 393224 | tf_op jit(solution)/shard_map/ppermute | solution.py:732
where the time goes:
time: 154 us; the launch traced here: 153 us
  Pallas kernels  69.4 us (45%)
  waiting for transfers between devices  48.4 us (31%)
  starting transfers between devices  27.1 us (18%)
  local copies, waits for them, and re-layouts  3.83 us (2%)
  other arithmetic  2.45 us (2%)
  between operations  2.05 us (1%)
    pallas_call x4, Pallas kernels, node_inner(): pl.pallas_call(kernel, grid=(count,), in_specs=in_specs, out_specs=[pl.Bl...  27.6 us
    all_to_all x4, waiting for transfers between devices, swap(): lax.all_to_all(v.reshape(half, state // half, v.shape[-1]), 'node', split...  25.2 us
    ppermute x4, waiting for transfers between devices, cross(): return lax.ppermute(v, 'node', across)  21.6 us
    all_to_all x4, starting transfers between devices, swap(): lax.all_to_all(v.reshape(half, state // half, v.shape[-1]), 'node', split...  19.6 us
    pallas_call x2, Pallas kernels, node_outer(): pl.pallas_call(functools.partial(outer_kernel, heads, head_width, chunk,...  17.9 us
    pallas_call x2, Pallas kernels, node_states(): pl.pallas_call(functools.partial(states_kernel, heads, head_width, chunk,...  11.1 us
    pallas_call x2, Pallas kernels, join_slots(): pl.pallas_call(kernel, in_specs=in_specs, out_specs=pl.BlockSpec(memory_s...  7.7 us
    ppermute x4, starting transfers between devices, cross(): return lax.ppermute(v, 'node', across)  7.44 us
  transfers between devices with their start and end apart: 9, of which 6 were waited for; matrix products, arithmetic and copies ran while one was open for 1% of the time, Pallas kernels for 33%

commit v1 on v0

--- a/solution.py
+++ b/solution.py
@@ -302,7 +302,7 @@
 def node_inner(x, cot, b, c, gram, low, src, prior, chunk, part, parts, heads, head_width):
     length, state = b.shape
     width = heads * head_width
-    block = min(width // parts, 2 * LANES)
+    block = min(width // parts, 4 * LANES)
     count = width // block // parts
     offset = (chunk * parts + part) * count
     whole = lambda i: (0, 0)
@@ -785,8 +785,7 @@
     packed = []
     for k in range(CHUNKS):
         main, *more = pack_slots(parents, received[k], nodes, *sizes)
-        held = pltpu.with_memory_space_constraint(main, pltpu.HBM)
-        packed.append((cross(held), more))
+        packed.append((cross(main), more))
     others = lax.switch(
         crowded,
         (

time: 154 us -> 151 us (0.981)
  Pallas kernels: 69.4 us -> 67.5 us
where the time goes in v1:
time: 151 us; the launch traced here: 150 us
  Pallas kernels  67.5 us (45%)
  waiting for transfers between devices  48.9 us (32%)
  starting transfers between devices  27 us (18%)
  other arithmetic  2.44 us (2%)
  local copies, waits for them, and re-layouts  2.3 us (2%)
  between operations  1.88 us (1%)
    pallas_call x4, Pallas kernels, node_inner(): pl.pallas_call(kernel, grid=(count,), in_specs=in_specs, out_specs=[pl.Bl...  26.3 us
    all_to_all x4, waiting for transfers between devices, swap(): lax.all_to_all(v.reshape(half, state // half, v.shape[-1]), 'node', split...  25.4 us
    ppermute x4, waiting for transfers between devices, cross(): return lax.ppermute(v, 'node', across)  21.9 us
    all_to_all x4, starting transfers between devices, swap(): lax.all_to_all(v.reshape(half, state // half, v.shape[-1]), 'node', split...  19.5 us
    pallas_call x2, Pallas kernels, node_outer(): pl.pallas_call(functools.partial(outer_kernel, heads, head_width, chunk,...  18 us
    pallas_call x2, Pallas kernels, node_states(): pl.pallas_call(functools.partial(states_kernel, heads, head_width, chunk,...  11.1 us
    ppermute x4, starting transfers between devices, cross(): return lax.ppermute(v, 'node', across)  7.42 us
    pallas_call x2, Pallas kernels, join_slots(): pl.pallas_call(kernel, in_specs=in_specs, out_specs=pl.BlockSpec(memory_s...  7.09 us
  transfers between devices with their start and end apart: 9, of which 6 were waited for; matrix products, arithmetic and copies ran while one was open for 1% of the time, Pallas kernels for 33%

profile of v1, /device:TPU:0, one launch (start us, length us, event | category | flops | bytes accessed | tf_op | source)
XLA Modules:
  0.0 150.1 jit_solution(4032723447087285723)
XLA Ops:
  0.6 5.4 %node_states.3 = (bf16[128,4224]{1,0:T(8,128)(2,1)}, f32[512,128]{1,0:T(8,128)}, f32[32,512]{1,0:T(8,128)}, bf16[512,128]{1,0:T(8,128)(2,1)}, bf16[512,128]{1,0:...) custom-call(bf16[512,4096]{1,0:T(8,128)(2,1)} %refs_7_.1, ...), custom_call_target="tpu_custom_call" | custom-call | flops 536870912 | bytes 6291456 | tf_op jit(solution)/shard_map/node_states/pallas_call | solution.py:185
  6.1 6.2 %all-to-all-start = ((bf16[8,16,4224]{2,1,0:T(8,128)(2,1)}), bf16[8,16,4224]{2,1,0:T(8,128)(2,1)S(1)}, u32[]{:S(2)}, u32[]{:S(2)}) async-start(bf16[8,16,4224]{2,1,0:T(8,128)(2,1)} %bitcast.18), calls=%async_computation | async-start | bytes 2162688 | tf_op jit(solution)/shard_map/all_to_all | solution.py:749
  12.3 5.6 %node_states.2 = (bf16[128,4224]{1,0:T(8,128)(2,1)}, f32[512,128]{1,0:T(8,128)}, f32[32,512]{1,0:T(8,128)}, bf16[512,128]{1,0:T(8,128)(2,1)}, bf16[512,128]{1,0:...) custom-call(bf16[512,4096]{1,0:T(8,128)(2,1)} %refs_7_.1, ...), custom_call_target="tpu_custom_call" | custom-call | flops 536870912 | bytes 6291456 | tf_op jit(solution)/shard_map/node_states/pallas_call | solution.py:185
  17.9 9.4 %all-to-all-done.recv_ref = bf16[8,16,4224]{2,1,0:T(8,128)(2,1)S(1)} async-done(((bf16[8,16,4224]{2,1,0:T(8,128)(2,1)}), bf16[8,16,4224]{2,1,0:T(8,128)(2,1)S(1)}, u32[]{:S(2)}, u32[]{:S(2)}) %all-to-all-start) | async-done | bytes 1081376 | tf_op jit(solution)/shard_map/all_to_all | solution.py:749
  27.4 3.6 %all-to-all-start.1 = ((bf16[8,16,4224]{2,1,0:T(8,128)(2,1)}), bf16[8,16,4224]{2,1,0:T(8,128)(2,1)S(1)}, u32[]{:S(2)}, u32[]{:S(2)}) async-start(bf16[8,16,4224]{2,1,0:T(8,128)(2,1)} %bitcast.17), calls=%async_computation.1 | async-start | bytes 2162688 | tf_op jit(solution)/shard_map/all_to_all | solution.py:749
  30.9 2.5 %pack_slots.2 = (bf16[6,16,2176]{2,1,0:T(8,128)(2,1)S(1)}, bf16[2,16,2176]{2,1,0:T(8,128)(2,1)}, bf16[4,16,2176]{2,1,0:T(8,128)(2,1)}) custom-call(s32[16]{0:T(128)S(1)} %copy-done, bf16[8,16,4224]{2,1,0:T(8,128)(2,1)S(1)} %all-to-all-done.recv_ref), custom_call_target="tpu_custom_call" | custom-call | flops 5242880 | bytes 2097152 | tf_op jit(solution)/shard_map/pack_slots/pallas_call | solution.py:470
  33.5 2.7 %collective-permute-start.6 = (bf16[6,16,2176]{2,1,0:T(8,128)(2,1)S(1)}, bf16[6,16,2176]{2,1,0:T(8,128)(2,1)S(1)}, u32[]{:S(2)}, u32[]{:S(2)}) collective-permute-start(bf16[6,16,2176]{2,1,0:T(8,128)(2,1)S(1)} %get-tuple-element.114), channel_id=1, source_target_pairs={{0,16},{2,18},{4,20},{6,22},{8,24},{10,26},{12,28},{14,30},{16,0},... | collective-permute-start | bytes 1253384 | tf_op jit(solution)/shard_map/ppermute | solution.py:759
  36.2 0.1 fusion.3
  36.3 0.6 convert_reduce_fusion
  38.0 16.0 %all-to-all-done.1.recv_ref = bf16[8,16,4224]{2,1,0:T(8,128)(2,1)S(1)} async-done(((bf16[8,16,4224]{2,1,0:T(8,128)(2,1)}), bf16[8,16,4224]{2,1,0:T(8,128)(2,1)S(1)}, u32[]{:S(2)}, u32[]{:S(2)}) %all-to-all-start.1) | async-done | bytes 1081376 | tf_op jit(solution)/shard_map/all_to_all | solution.py:749
  54.1 2.5 %pack_slots.3 = (bf16[6,16,2176]{2,1,0:T(8,128)(2,1)S(1)}, bf16[2,16,2176]{2,1,0:T(8,128)(2,1)}, bf16[4,16,2176]{2,1,0:T(8,128)(2,1)}) custom-call(s32[16]{0:T(128)S(1)} %copy-done, bf16[8,16,4224]{2,1,0:T(8,128)(2,1)S(1)} %all-to-all-done.1.recv_ref), custom_call_target="tpu_custom_call" | custom-call | flops 5242880 | bytes 2097152 | tf_op jit(solution)/shard_map/pack_slots/pallas_call | solution.py:470
  56.6 13.7 %conditional.1 = ((bf16[2,16,2176]{2,1,0:T(8,128)(2,1)}, bf16[4,16,2176]{2,1,0:T(8,128)(2,1)}, bf16[2,16,2176]{2,1,0:T(8,128)(2,1)}, bf16[4,16,2176]{2,1,0:T(8,128)(2,1)})) conditional(s32[]{:T(128)} %clamp.3, (bf16[2,16,2176]{2,1,0:T(8,128)(2,1)}, bf16[4,16,2176]{2,1,0:T(8,128)(2,1)}, bf16[2,16,2176]{2,1,0:T(8,128)(2,1)}, ...), branch_computations={%region_2.0_spmd, %region_3.0_spmd, %region_4.0_spmd} | conditional | bytes 5013704 | solution.py:789
  56.6 2.9 %collective-permute-start.1 = (bf16[2,16,2176]{2,1,0:T(8,128)(2,1)}, bf16[2,16,2176]{2,1,0:T(8,128)(2,1)S(1)}, u32[]{:S(2)}, u32[]{:S(2)}) collective-permute-start(bf16[2,16,2176]{2,1,0:T(8,128)(2,1)} %get-tuple-element.26), channel_id=1, source_target_pairs={{0,16},{2,18},{4,20},{6,22},{8,24},{10,26},{12,28},{14,30},{16,0},... | collective-permute-start | bytes 417800 | tf_op jit(solution)/shard_map/cond/branch_1_fun/ppermute | solution.py:759
  59.5 7.3 %collective-permute-done = bf16[2,16,2176]{2,1,0:T(8,128)(2,1)S(1)} collective-permute-done((bf16[2,16,2176]{2,1,0:T(8,128)(2,1)}, bf16[2,16,2176]{2,1,0:T(8,128)(2,1)S(1)}, u32[]{:S(2)}, u32[]{:S(2)}) %collective-permute-start) | collective-permute-done | bytes 139296 | tf_op jit(solution)/shard_map/cond/branch_1_fun/ppermute | solution.py:759
  66.8 0.6 copy.29
  67.5 2.3 %collective-permute-done.1 = bf16[2,16,2176]{2,1,0:T(8,128)(2,1)S(1)} collective-permute-done((bf16[2,16,2176]{2,1,0:T(8,128)(2,1)}, bf16[2,16,2176]{2,1,0:T(8,128)(2,1)S(1)}, u32[]{:S(2)}, u32[]{:S(2)}) %collective-permute-start.1) | collective-permute-done | bytes 139296 | tf_op jit(solution)/shard_map/cond/branch_1_fun/ppermute | solution.py:759
  69.7 0.7 copy.31
  70.4 3.8 %join_slots.2 = bf16[8,16,4096]{2,1,0:T(8,128)(2,1)} custom-call(s32[16]{0:T(128)S(1)} %copy-done, bf16[8,16,4224]{2,1,0:T(8,128)(2,1)S(1)} %all-to-all-done.recv_ref, bf16[6,16,2176]{2,1,0:T(8,128)(2,1)S(1)} %collective-permute-done.6.refs_0_, bf16[2,16,2176]{2,1,0:T(8,128)(2,1)} %get-tuple-element.120.refs_1_, bf16[4,16,2176]{2,1,0:T(8,128)(2,1)} %get-tuple-element.121.refs_2_), custom_call_target="tpu_custom_call" | custom-call | flops 5242880 | bytes 2097152 | tf_op jit(solution)/shard_map/join_slots/pallas_call | solution.py:571
  74.2 3.6 %all-to-all-start.2 = ((bf16[8,16,4096]{2,1,0:T(8,128)(2,1)}), bf16[8,16,4096]{2,1,0:T(8,128)(2,1)S(1)}, u32[]{:S(2)}, u32[]{:S(2)}) async-start(bf16[8,16,4096]{2,1,0:T(8,128)(2,1)} %join_slots.2), calls=%async_computation.2 | async-start | bytes 2097152 | tf_op jit(solution)/shard_map/all_to_all | solution.py:749
  77.8 1.8 %collective-permute-start.7 = (bf16[6,16,2176]{2,1,0:T(8,128)(2,1)S(1)}, bf16[6,16,2176]{2,1,0:T(8,128)(2,1)S(1)}, u32[]{:S(2)}, u32[]{:S(2)}) collective-permute-start(bf16[6,16,2176]{2,1,0:T(8,128)(2,1)S(1)} %get-tuple-element.125), channel_id=1, source_target_pairs={{0,16},{2,18},{4,20},{6,22},{8,24},{10,26},{12,28},{14,30},{16,0},... | collective-permute-start | bytes 1253384 | tf_op jit(solution)/shard_map/ppermute | solution.py:759
  79.6 6.6 %node_inner.4 = (bf16[512,4096]{1,0:T(8,128)(2,1)}, bf16[512,4096]{1,0:T(8,128)(2,1)}, f32[512,128]{1,0:T(8,128)}, f32[512,128]{1,0:T(8,128)}) custom-call(bf16[512,4096]{1,0:T(8,128)(2,1)} %refs_7_.1, bf16[512,4096]{1,0:T(8,128)(2,1)} %refs_8_.1, bf16[512,128]{1,0:T(8,128)(2,1)} %refs_0_.7, bf16[512,128]{1,0:T(8,128)(2,1)} %refs_1_.7, ...), custom_call_target="tpu_custom_call" | custom-call | flops 6442450944 | bytes 6291456 | tf_op jit(solution)/shard_map/node_inner/pallas_call | solution.py:327
  86.2 12.4 %collective-permute-done.7.refs_0_ = bf16[6,16,2176]{2,1,0:T(8,128)(2,1)S(1)} collective-permute-done((bf16[6,16,2176]{2,1,0:T(8,128)(2,1)S(1)}, bf16[6,16,2176]{2,1,0:T(8,128)(2,1)S(1)}, u32[]{:S(2)}, u32[]{:S(2)}) %collective-permute-start.7) | collective-permute-done | bytes 417824 | tf_op jit(solution)/shard_map/ppermute | solution.py:759
  98.6 3.3 %join_slots.3 = bf16[8,16,4096]{2,1,0:T(8,128)(2,1)} custom-call(s32[16]{0:T(128)S(1)} %copy-done, bf16[8,16,4224]{2,1,0:T(8,128)(2,1)S(1)} %all-to-all-done.1.recv_ref, bf16[6,16,2176]{2,1,0:T(8,128)(2,1)S(1)} %collective-permute-done.7.refs_0_, bf16[2,16,2176]{2,1,0:T(8,128)(2,1)S(1)} %copy-done.4, bf16[4,16,2176]{2,1,0:T(8,128)(2,1)S(1)} %copy-done.3), custom_call_target="tpu_custom_call" | custom-call | flops 5242880 | bytes 2097152 | tf_op jit(solution)/shard_map/join_slots/pallas_call | solution.py:571
  101.9 6.1 %all-to-all-start.3 = ((bf16[8,16,4096]{2,1,0:T(8,128)(2,1)}), bf16[8,16,4096]{2,1,0:T(8,128)(2,1)S(1)}, u32[]{:S(2)}, u32[]{:S(2)}) async-start(bf16[8,16,4096]{2,1,0:T(8,128)(2,1)} %join_slots.3), calls=%async_computation.3 | async-start | bytes 2097152 | tf_op jit(solution)/shard_map/all_to_all | solution.py:749
  108.0 6.6 %node_inner.5 = (bf16[512,4096]{1,0:T(8,128)(2,1)}, bf16[512,4096]{1,0:T(8,128)(2,1)}, f32[512,128]{1,0:T(8,128)}, f32[512,128]{1,0:T(8,128)}) custom-call(bf16[512,4096]{1,0:T(8,128)(2,1)} %refs_7_.1, bf16[512,4096]{1,0:T(8,128)(2,1)} %refs_8_.1, bf16[512,128]{1,0:T(8,128)(2,1)} %refs_0_.7, ...), custom_call_target="tpu_custom_call", output_to_operand_aliasing={{0}: (7, {}), {1}: (8, {})} | custom-call | flops 6442450944 | bytes 6291456 | tf_op jit(solution)/shard_map/node_inner/pallas_call | solution.py:327
  114.6 6.6 %node_inner.6 = (bf16[512,4096]{1,0:T(8,128)(2,1)}, bf16[512,4096]{1,0:T(8,128)(2,1)}, f32[512,128]{1,0:T(8,128)}, f32[512,128]{1,0:T(8,128)}) custom-call(bf16[512,4096]{1,0:T(8,128)(2,1)} %refs_7_.1, bf16[512,4096]{1,0:T(8,128)(2,1)} %refs_8_.1, bf16[512,128]{1,0:T(8,128)(2,1)} %refs_0_.7, ...), custom_call_target="tpu_custom_call", output_to_operand_aliasing={{0}: (7, {}), {1}: (8, {})} | custom-call | flops 6442450944 | bytes 6291456 | tf_op jit(solution)/shard_map/node_inner/pallas_call | solution.py:327
  121.2 6.6 %node_inner.7 = (bf16[512,4096]{1,0:T(8,128)(2,1)}, bf16[512,4096]{1,0:T(8,128)(2,1)}, f32[512,128]{1,0:T(8,128)}, f32[512,128]{1,0:T(8,128)}) custom-call(bf16[512,4096]{1,0:T(8,128)(2,1)} %refs_7_.1, bf16[512,4096]{1,0:T(8,128)(2,1)} %refs_8_.1, bf16[512,128]{1,0:T(8,128)(2,1)} %refs_0_.7, ...), custom_call_target="tpu_custom_call", output_to_operand_aliasing={{0}: (7, {}), {1}: (8, {})} | custom-call | flops 6442450944 | bytes 6291456 | tf_op jit(solution)/shard_map/node_inner/pallas_call | solution.py:327
  127.8 9.1 %node_outer.2 = (bf16[512,4096]{1,0:T(8,128)(2,1)}, bf16[512,4096]{1,0:T(8,128)(2,1)}, f32[512,128]{1,0:T(8,128)}, f32[512,128]{1,0:T(8,128)}) custom-call(bf16[512,128]{1,0:T(8,128)(2,1)} %refs_0_.7, bf16[512,128]{1,0:T(8,128)(2,1)} %refs_1_.7, bf16[512,128]{1,0:T(8,128)(2,1)} %get-tuple-element.89.refs_2_, bf16[512,128]{1,0:T(8,128)(2,1)} %get-tuple-element.90.refs_3_, ...), custom_call_target="tpu_custom_call" | custom-call | flops 1073741824 | bytes 14680064 | tf_op jit(solution)/shard_map/node_outer/pallas_call | solution.py:712
  136.9 1.0 copy-done.2
  137.9 8.9 %node_outer.3 = (bf16[512,4096]{1,0:T(8,128)(2,1)}, bf16[512,4096]{1,0:T(8,128)(2,1)}, f32[256,128]{1,0:T(8,128)}, f32[256,128]{1,0:T(8,128)}, bf16[2,256,128]{2,1,0:T(8,128)(2,1)}) custom-call(bf16[512,128]{1,0:T(8,128)(2,1)} %refs_0_.7, bf16[512,128]{1,0:T(8,128)(2,1)} %refs_1_.7, ...), custom_call_target="tpu_custom_call", output_to_operand_aliasing={{0}: (15, {}), {1}: (16, {})} | custom-call | flops 1073741824 | bytes 14680064 | tf_op jit(solution)/shard_map/node_outer/pallas_call | solution.py:712
  146.8 1.5 %collective-permute-done.8 = bf16[2,256,128]{2,1,0:T(8,128)(2,1)S(1)} collective-permute-done((bf16[2,256,128]{2,1,0:T(8,128)(2,1)}, bf16[2,256,128]{2,1,0:T(8,128)(2,1)S(1)}, u32[]{:S(2)}, u32[]{:S(2)}) %collective-permute-start.8) | collective-permute-done | bytes 131104 | tf_op jit(solution)/shard_map/ppermute | solution.py:732
  148.4 1.7 %fusion = (f32[256,128]{1,0:T(8,128)}, f32[256,128]{1,0:T(8,128)}) fusion(f32[256,128]{1,0:T(8,128)} %get-tuple-element.135, f32[2,256,128]{2,1,0:T(8,128)S(1)} %convert_element_type.15, f32[256,128]{1,0:T(8,128)} %get-tuple-element.133), kind=kLoop, calls=%fused_computation.1 | loop fusion | flops 65536 | bytes 786432 | tf_op jit(solution)/shard_map/add | solution.py:733
  (16 shorter events, 0.1 us)
Async XLA Ops:
  6.1 21.3 %all-to-all-start = ((bf16[8,16,4224]{2,1,0:T(8,128)(2,1)}), bf16[8,16,4224]{2,1,0:T(8,128)(2,1)S(1)}, u32[]{:S(2)}, u32[]{:S(2)}) async-start(bf16[8,16,4224]{2,1,0:T(8,128)(2,1)} %bitcast.18), calls=%async_computation | async-start | bytes 2162688 | tf_op jit(solution)/shard_map/all_to_all | solution.py:749
  12.3 18.6 %copy-start = (s32[16]{0:T(128)S(1)}, s32[16]{0:T(128)}, u32[]{:S(2)}) copy-start(s32[16]{0:T(128)} %parents_ref.7) | copy-start | bytes 196
  27.4 26.7 %all-to-all-start.1 = ((bf16[8,16,4224]{2,1,0:T(8,128)(2,1)}), bf16[8,16,4224]{2,1,0:T(8,128)(2,1)S(1)}, u32[]{:S(2)}, u32[]{:S(2)}) async-start(bf16[8,16,4224]{2,1,0:T(8,128)(2,1)} %bitcast.17), calls=%async_computation.1 | async-start | bytes 2162688 | tf_op jit(solution)/shard_map/all_to_all | solution.py:749
  33.5 36.9 %collective-permute-start.6 = (bf16[6,16,2176]{2,1,0:T(8,128)(2,1)S(1)}, bf16[6,16,2176]{2,1,0:T(8,128)(2,1)S(1)}, u32[]{:S(2)}, u32[]{:S(2)}) collective-permute-start(bf16[6,16,2176]{2,1,0:T(8,128)(2,1)S(1)} %get-tuple-element.114), channel_id=1, source_target_pairs={{0,16},{2,18},{4,20},{6,22},{8,24},{10,26},{12,28},{14,30},{16,0},... | collective-permute-start | bytes 1253384 | tf_op jit(solution)/shard_map/ppermute | solution.py:759
  56.6 10.2 %collective-permute-start = (bf16[2,16,2176]{2,1,0:T(8,128)(2,1)}, bf16[2,16,2176]{2,1,0:T(8,128)(2,1)S(1)}, u32[]{:S(2)}, u32[]{:S(2)}) collective-permute-start(bf16[2,16,2176]{2,1,0:T(8,128)(2,1)} %get-tuple-element.24), channel_id=1, source_target_pairs={{0,16},{2,18},{4,20},{6,22},{8,24},{10,26},{12,28},{14,30},{16,0},... | collective-permute-start | bytes 417800 | tf_op jit(solution)/shard_map/cond/branch_1_fun/ppermute | solution.py:759
  56.6 13.1 %collective-permute-start.1 = (bf16[2,16,2176]{2,1,0:T(8,128)(2,1)}, bf16[2,16,2176]{2,1,0:T(8,128)(2,1)S(1)}, u32[]{:S(2)}, u32[]{:S(2)}) collective-permute-start(bf16[2,16,2176]{2,1,0:T(8,128)(2,1)} %get-tuple-element.26), channel_id=1, source_target_pairs={{0,16},{2,18},{4,20},{6,22},{8,24},{10,26},{12,28},{14,30},{16,0},... | collective-permute-start | bytes 417800 | tf_op jit(solution)/shard_map/cond/branch_1_fun/ppermute | solution.py:759
  74.2 27.7 %all-to-all-start.2 = ((bf16[8,16,4096]{2,1,0:T(8,128)(2,1)}), bf16[8,16,4096]{2,1,0:T(8,128)(2,1)S(1)}, u32[]{:S(2)}, u32[]{:S(2)}) async-start(bf16[8,16,4096]{2,1,0:T(8,128)(2,1)} %join_slots.2), calls=%async_computation.2 | async-start | bytes 2097152 | tf_op jit(solution)/shard_map/all_to_all | solution.py:749
  77.8 20.8 %collective-permute-start.7 = (bf16[6,16,2176]{2,1,0:T(8,128)(2,1)S(1)}, bf16[6,16,2176]{2,1,0:T(8,128)(2,1)S(1)}, u32[]{:S(2)}, u32[]{:S(2)}) collective-permute-start(bf16[6,16,2176]{2,1,0:T(8,128)(2,1)S(1)} %get-tuple-element.125), channel_id=1, source_target_pairs={{0,16},{2,18},{4,20},{6,22},{8,24},{10,26},{12,28},{14,30},{16,0},... | collective-permute-start | bytes 1253384 | tf_op jit(solution)/shard_map/ppermute | solution.py:759
  79.6 19.0 %copy-start.3 = (bf16[4,16,2176]{2,1,0:T(8,128)(2,1)S(1)}, bf16[4,16,2176]{2,1,0:T(8,128)(2,1)}, u32[]{:S(2)}) copy-start(bf16[4,16,2176]{2,1,0:T(8,128)(2,1)} %get-tuple-element.127.refs_2_) | copy-start | bytes 835588
  79.6 19.0 %copy-start.4 = (bf16[2,16,2176]{2,1,0:T(8,128)(2,1)S(1)}, bf16[2,16,2176]{2,1,0:T(8,128)(2,1)}, u32[]{:S(2)}) copy-start(bf16[2,16,2176]{2,1,0:T(8,128)(2,1)} %get-tuple-element.126.refs_1_) | copy-start | bytes 417796
  101.9 12.7 %copy-start.1 = (bf16[8,16,4096]{2,1,0:T(8,128)(2,1)}, bf16[8,16,4096]{2,1,0:T(8,128)(2,1)S(1)}, u32[]{:S(2)}) copy-start(bf16[8,16,4096]{2,1,0:T(8,128)(2,1)S(1)} %all-to-all-done.2) | copy-start | bytes 3145732
  101.9 35.0 %all-to-all-start.3 = ((bf16[8,16,4096]{2,1,0:T(8,128)(2,1)}), bf16[8,16,4096]{2,1,0:T(8,128)(2,1)S(1)}, u32[]{:S(2)}, u32[]{:S(2)}) async-start(bf16[8,16,4096]{2,1,0:T(8,128)(2,1)} %join_slots.3), calls=%async_computation.3 | async-start | bytes 2097152 | tf_op jit(solution)/shard_map/all_to_all | solution.py:749
  136.9 1.0 copy-start.2
  146.8 1.6 %collective-permute-start.8 = (bf16[2,256,128]{2,1,0:T(8,128)(2,1)}, bf16[2,256,128]{2,1,0:T(8,128)(2,1)S(1)}, u32[]{:S(2)}, u32[]{:S(2)}) collective-permute-start(bf16[2,256,128]{2,1,0:T(8,128)(2,1)} %get-tuple-element.134), channel_id=1, source_target_pairs={{0,1},{1,0},{2,3},{3,2},{4,5},{5,4},{6,7},{7,6},{8,9},{9,8},{10,11... | collective-permute-start | bytes 393224 | tf_op jit(solution)/shard_map/ppermute | solution.py:732
